TPU v7x, 256 devices: a whole 4x4x8 slice. The times are simulated.
256 devices in a mesh: rows: 8 (over y, x_hi), weeks: 32 (over z, x_lo, core).
Axes of the slice: x: 4 (x_hi: 2, x_lo: 2; x = x_hi * 2 + x_lo), y: 4, z: 8, core: 2. Of those that a mesh axis runs over, the one named last changes fastest.
Arguments:
- counts: int32 [32768, 4096], P('rows', 'weeks'), may hold values from 0 to 15
- offsets: bfloat16 [32768, 4096], P('rows', 'weeks'), may hold values from -1.2 to 2.52
- loadings: float32 [32768, 64], P('rows'), may hold values from -0.4 to 0.4
- factors: float32 [4096, 64], P('weeks'), may hold values from -0.4 to 0.4
Outputs:
- new_loadings: float32 [32768, 64], P('rows')
- new_factors: float32 [4096, 64], P('weeks')
All inputs are finite; a program needn't handle non-finite values.
Results may differ from a plain program's by a relative error of at most 0.0003.
Values sent between devices are 32-bit elements; how exact they have to be, the bound alone decides.
A program may use at most 64 MiB of HBM per device.

v0:
```python
import jax
import jax.numpy as jnp
from jax import lax
from jax.sharding import PartitionSpec as P

ITERS = 2


HIGH = lax.Precision.HIGHEST


def residuals(counts_f, offsets_f, load, fac):
    eta = offsets_f + jnp.dot(load, fac.T, precision=HIGH)
    mu_val = jnp.exp(eta)
    return (counts_f - mu_val, mu_val)


def left_terms(resid, mu_val, fac):
    grad_a = jnp.dot(resid, fac, precision=HIGH)
    curv_a = jnp.dot(mu_val, fac * fac, precision=HIGH)
    return jnp.concatenate((grad_a, curv_a), 1)


def right_terms(resid, mu_val, load):
    dims = (((0,), (0,)), ((), ()))
    grad_b = lax.dot_general(resid, load, dims, precision=HIGH)
    curv_b = lax.dot_general(mu_val, load * load, dims, precision=HIGH)
    return jnp.concatenate((grad_b, curv_b), 1)


def apply_step(value, stacked):
    width = value.shape[1]
    return value + stacked[:, :width] / (1.0 + stacked[:, width:])


def local(counts, offsets, loadings, factors):
    counts_f = counts.astype(jnp.float32)
    offsets_f = offsets.astype(jnp.float32)
    load = loadings
    fac = factors
    for step in range(ITERS):
        resid, mu_val = residuals(counts_f, offsets_f, load, fac)
        stacked_a = left_terms(resid, mu_val, fac)
        total_a = lax.psum(stacked_a, "weeks")
        load = apply_step(load, total_a)
        resid, mu_val = residuals(counts_f, offsets_f, load, fac)
        stacked_b = right_terms(resid, mu_val, load)
        total_b = lax.psum(stacked_b, "rows")
        fac = apply_step(fac, total_b)
    return (load, fac)


def solution(mesh):
    placed = (P("rows", "weeks"), P("rows", "weeks"), P("rows", None), P("weeks", None))
    return jax.shard_map(
        local,
        mesh=mesh,
        in_specs=placed,
        out_specs=(P("rows", None), P("weeks", None)),
        check_vma=False,
    )
```

profile of v0, /device:TPU:1, one launch (start us, length us, event | category | flops | bytes accessed | tf_op | source)
XLA Modules:
  0.0 692.5 jit_solution(8604588127180002384)
XLA Ops:
  7.2 0.0 all-reduce.5.cloned.1.call-start
  7.2 5.0 fusion.3
  12.3 2.4 fusion.30
  14.7 2.5 fusion.10
  17.2 1.5 pad_maximum_fusion
  18.7 0.0 all-reduce.5.cloned.1.call-update
  18.7 0.2 all-reduce.7.cloned.1.call-start
  19.0 234.0 %all-reduce.5.cloned.1.call-done = f32[4096,128]{0,1:T(8,128)} async-done(((f32[4096,128]{0,1:T(8,128)}), f32[4096,128]{0,1:T(8,128)}) %all-reduce.5.cloned.1.call-update) | async-done | bytes 2097168 | tf_op jit(solution)/shard_map/psum | solution.py:44
  253.0 2.0 fusion.19
  255.0 4.7 fusion.2
  259.7 1.5 fusion.22
  261.2 1.6 fusion.8
  262.8 0.6 pad_maximum_fusion.2
  263.5 0.0 all-reduce.7.cloned.1.call-update
  263.5 0.3 all-reduce.9.cloned.1.call-start
  263.8 82.8 %all-reduce.7.cloned.1.call-done = f32[128,128]{0,1:T(8,128)} async-done(((f32[128,128]{0,1:T(8,128)}), f32[128,128]{0,1:T(8,128)}) %all-reduce.7.cloned.1.call-update) | async-done | bytes 65552 | tf_op jit(solution)/shard_map/psum | solution.py:48
  346.6 0.8 fusion.27
  347.4 4.7 fusion.1
  352.1 2.4 fusion.28
  354.5 2.5 fusion.6
  357.0 1.5 pad_maximum_fusion.1
  358.5 0.3 all-reduce.11.cloned.1.call-start
  358.8 233.5 %all-reduce.9.cloned.1.call-done = f32[4096,128]{0,1:T(8,128)} async-done(((f32[4096,128]{0,1:T(8,128)}), f32[4096,128]{0,1:T(8,128)}) %all-reduce.9.cloned.1.call-update) | async-done | bytes 2097168 | tf_op jit(solution)/shard_map/psum | solution.py:44
  592.3 1.8 fusion.17
  594.1 0.1 copy-done.2
  594.2 3.4 fusion
  597.6 1.5 fusion.20
  599.1 1.7 fusion.4
  600.8 0.6 pad_maximum_fusion.3
  601.4 0.0 all-reduce.11.cloned.1.call-update
  601.5 83.1 %all-reduce.11.cloned.1.call-done = f32[128,128]{0,1:T(8,128)} async-done(((f32[128,128]{0,1:T(8,128)}), f32[128,128]{0,1:T(8,128)}) %all-reduce.11.cloned.1.call-update) | async-done | bytes 65552 | tf_op jit(solution)/shard_map/psum | solution.py:48
  684.6 1.4 fusion.25
  (8 shorter events, 0.0 us)
Async XLA Ops:
  7.2 5.1 copy-start.3
  7.2 245.8 %all-reduce.5.cloned.1.call-start = ((), (), s32[]{:S(2)}) async-start(), calls=%async_computation | async-start | bytes 4194304 | tf_op jit(solution)/shard_map/psum | solution.py:44
  12.3 2.4 copy-start
  18.7 327.9 %all-reduce.7.cloned.1.call-start = ((), (), s32[]{:S(2)}) async-start(), calls=%async_computation.1 | async-start | bytes 131072 | tf_op jit(solution)/shard_map/psum | solution.py:48
  263.5 328.8 %all-reduce.9.cloned.1.call-start = ((), (), s32[]{:S(2)}) async-start(), calls=%async_computation.2 | async-start | bytes 4194304 | tf_op jit(solution)/shard_map/psum | solution.py:44
  358.5 326.1 %all-reduce.11.cloned.1.call-start = ((), (), s32[]{:S(2)}) async-start(), calls=%async_computation.3 | async-start | bytes 131072 | tf_op jit(solution)/shard_map/psum | solution.py:48
  592.3 1.9 copy-start.2
  594.2 5.0 copy-start.1
Sparse Core Ops, SparseCore 0:
  18.8 234.0 all-reduce.4
  263.6 82.9 all-reduce.6
  358.6 233.6 all-reduce.8
  601.6 82.9 all-reduce.10
where the time goes:
time: 697 us; the launch traced here: 693 us
  waiting for transfers between devices  634 us (91%)
  matrix products  34.1 us (5%)
  between operations  13.8 us (2%)
  other arithmetic  10.2 us (1%)
    psum x2, waiting for transfers between devices, local(): total_a = lax.psum(stacked_a, 'weeks')  468 us
    psum x2, waiting for transfers between devices, local(): total_b = lax.psum(stacked_b, 'rows')  166 us
    dot_general x4, matrix products, residuals(): eta = offsets_f + jnp.dot(load, fac.T, precision=HIGH)  17.9 us
  transfers between devices with their start and end apart: 4, of which 4 were waited for; matrix products, arithmetic and copies ran while one was open for 0% of the time, Pallas kernels for 0%

commit v1 on v0

v1 whole, which is shorter than its diff:
```python
import functools

import jax
import jax.numpy as jnp
from jax import lax
from jax.experimental import pallas as pl
from jax.experimental.pallas import tpu as pltpu
from jax.sharding import PartitionSpec as P

ITERS = 2
F32 = jnp.float32
BF16 = jnp.bfloat16
MESH = pl.DeviceIdType.MESH
NZ = 8
R = 8


def far_first(j):
    return 4 + (1 - 2 * lax.rem(j, 2)) * lax.div(j + 1, 2)


def split(v):
    hi = v.astype(BF16)
    lo = (v - hi.astype(F32)).astype(BF16)
    return hi, lo


def mm(a, b):
    return jnp.dot(a, b, preferred_element_type=F32)


def kernel(
    counts, offs, load, fac, at_out, fac_out,
    cnt, obf, off, osend, a0, xmat, weta, w1, w3, g1, g2,
    bt, at1, at2, xs, xr, so, zs, zr, gs, gr,
    s_loc, s_cnt, s_off, s_bt, s_send, s_x, s_z, s_agz, s_agx, s_g, s_b, s_sib, s_out,
):
    r = lax.axis_index("rows")
    w = lax.axis_index("weeks")
    z = lax.div(w, 4)
    xl = lax.rem(lax.div(w, 2), 2)
    c = lax.rem(w, 2)
    sib = (r, w + 1 - 2 * c)
    xp = (r, w + 2 - 4 * xl)
    own = xl * 8 + z

    def zdev(o):
        return (r, lax.rem(w + 4 * o, 32))

    def rdev(idx):
        return (lax.rem(idx, 8), w - c + lax.div(idx, 8))

    def zsrc(j):
        return lax.rem(z + 8 - far_first(j), 8)

    def remote(src, dst, ss, rs, dev):
        return pltpu.make_async_remote_copy(
            src_ref=src, dst_ref=dst, send_sem=ss, recv_sem=rs, device_id=dev, device_id_type=MESH
        )

    def wait_bytes(ref, sem):
        pltpu.make_async_copy(ref, ref, sem).wait()

    me = c * 8 + r
    barrier = pltpu.get_barrier_semaphore()

    def greet_z(j, carry):
        pl.semaphore_signal(barrier, inc=1, device_id=zdev(j), device_id_type=MESH)
        return carry

    def greet_r(t, carry):
        pl.semaphore_signal(barrier, inc=1, device_id=rdev(lax.rem(me + t, 16)), device_id_type=MESH)
        return carry

    ld_off = pltpu.make_async_copy(offs, obf, s_loc.at[0])
    ld_cnt = pltpu.make_async_copy(counts.at[c], cnt.at[c], s_loc.at[1])
    ld_a0 = pltpu.make_async_copy(load.at[c], a0, s_loc.at[2])
    ld_off.start()
    ld_a0.start()
    ld_cnt.start()
    lax.fori_loop(1, 8, greet_z, 0)
    lax.fori_loop(1, 16, greet_r, 0)
    pl.semaphore_signal(barrier, inc=1, device_id=xp, device_id_type=MESH)

    bt[0, c] = fac[...].T.reshape(8, 8, 128)
    ld_off.wait()
    pl.semaphore_wait(barrier, 23)

    remote(bt.at[0, c], bt.at[0, c], s_send.at[0], s_bt, sib).start()

    def swap(j, carry):
        d = lax.rem(z + far_first(j), 8)
        remote(counts.at[1 - c, :, d], cnt.at[c, :, d], s_send.at[1], s_cnt.at[j], sib).start()
        for x in range(2):
            osend[x, d] = obf[1 - c, x, d].astype(F32)
        remote(osend.at[:, d], off.at[c, :, d], s_send.at[2], s_off.at[j], sib).start()
        return carry

    lax.fori_loop(0, 8, swap, 0)

    def prepare(d, carry):
        for x in range(2):
            off[c, x, d] = obf[c, x, d].astype(F32)
        return carry

    lax.fori_loop(0, 8, prepare, 0)
    ld_a0.wait()

    def first_x(b, carry):
        hi, lo = split(a0[b])
        xmat[b] = jnp.concatenate([hi.astype(F32), lo.astype(F32)], axis=1).astype(BF16)
        return carry

    lax.fori_loop(0, 16, first_x, 0)
    ld_cnt.wait()

    def week_weights(it):
        b = jnp.concatenate([bt[it, 0].reshape(64, 128), bt[it, 1].reshape(64, 128)], axis=1)
        bh, bl = split(b)
        qh, ql = split(b * b)
        weta[...] = jnp.concatenate([bh, bh, bl, bl], axis=0)
        bh, bl, qh, ql = (v.astype(F32) for v in (bh, bl, qh, ql))
        w1[...] = jnp.concatenate([bh, -qh, bl, -ql], axis=0).T.astype(BF16)
        zero = jnp.zeros_like(qh)
        w3[...] = jnp.concatenate([zero, qh, zero, ql], axis=0).T.astype(BF16)

    def residual(x, d):
        xb = xmat[x * 8 + d]
        eta = mm(jnp.concatenate([xb, xb], axis=1), weta[...])
        o = jnp.concatenate([off[0, x, d], off[1, x, d]], axis=1)
        n = jnp.concatenate([cnt[0, x, d], cnt[1, x, d]], axis=1).astype(F32)
        res = n - jnp.exp(eta + o)
        rh, rl = split(res)
        return rh, rl, n.astype(BF16)

    def left(x, d):
        rh, rl, n = residual(x, d)
        o = mm(rh, w1[...]) + mm(n, w3[...])
        return o[:, :128] + o[:, 128:] + mm(rl, w1[:, :128])

    def right(at, x, d):
        a = at[x * 8 + d]
        hi, lo = split(a)
        ph, pw = split(a * a)
        xmat[x * 8 + d] = jnp.concatenate([hi.astype(F32), lo.astype(F32)], axis=0).T.astype(BF16)
        rh, rl, n = residual(x, d)
        lt = jnp.concatenate([hi, -ph, lo, -pw], axis=0)
        g1[...] += mm(lt, rh)
        g2[:128] += mm(lt[:128], rl)
        g2[128:] += mm(jnp.concatenate([ph, pw], axis=0), n)

    for it in range(ITERS):
        last = it == ITERS - 1
        at = at2.at[c] if last else at1
        if it == 0:
            pltpu.make_async_copy(bt.at[0, 1 - c], bt.at[0, 1 - c], s_bt).wait()
        week_weights(it)

        def a_step(j, carry, it=it):
            @pl.when(j < 8)
            def _():
                d = lax.rem(z + far_first(j), 8)
                if it == 0:
                    wait_bytes(cnt.at[1 - c, :, d], s_cnt.at[j])
                    wait_bytes(off.at[1 - c, :, d], s_off.at[j])
                xs[it, j] = left(1 - xl, d)
                remote(xs.at[it, j], xr.at[it, j], s_send.at[3], s_x.at[it, j], xp).start()
                so[j] = left(xl, d)

            @pl.when(j >= 3)
            def _():
                k = j - 3
                wait_bytes(xr.at[it, k], s_x.at[it, k])
                zs[it, k] = so[k] + xr[it, k]

                @pl.when(k < 7)
                def _():
                    remote(
                        zs.at[it, k], zr.at[it, k], s_send.at[4], s_z.at[it, k], zdev(far_first(k))
                    ).start()

            return carry

        lax.fori_loop(0, 11, a_step, 0)

        def z_sum(k, total, it=it):
            wait_bytes(zr.at[it, k], s_z.at[it, k])
            return total + zr[it, k]

        total = lax.fori_loop(0, 7, z_sum, zs[it, 7]).T
        old = a0[own].T if it == 0 else at1[own]
        at[own] = old + total[:64] / (1.0 + total[64:])

        remote(at.at[own], at.at[own], s_send.at[5], s_agx.at[it, 7], xp).start()

        def ag_send(j, carry, it=it, at=at):
            remote(at.at[own], at.at[own], s_send.at[6], s_agz.at[it, j], zdev(far_first(j))).start()
            return carry

        lax.fori_loop(0, 7, ag_send, 0)

        g1[...] = jnp.zeros_like(g1)
        g2[...] = jnp.zeros_like(g2)
        right(at, xl, z)

        def b_step(k, carry, it=it, at=at):
            @pl.when(k < 7)
            def _():
                d = zsrc(k)
                blk = at.at[xl * 8 + d]
                wait_bytes(blk, s_agz.at[it, k])
                remote(blk, blk, s_send.at[5], s_agx.at[it, k], xp).start()
                right(at, xl, d)

            @pl.when(k >= 2)
            def _():
                k2 = lax.rem(k + 5, 8)
                d = zsrc(k2)
                wait_bytes(at.at[(1 - xl) * 8 + d], s_agx.at[it, k2])
                right(at, 1 - xl, d)

            return carry

        lax.fori_loop(0, 10, b_step, 0)

        if last:
            remote(at2.at[c], at2.at[c], s_send.at[7], s_sib, sib).start()
            pltpu.make_async_copy(at2.at[c], at_out.at[c], s_out.at[0]).start()

        grad = g1[0:64] + g1[128:192] + g2[0:64]
        curv = g1[64:128] + g1[192:256] + g2[64:128] + g2[128:192] + g2[192:256]
        for h in range(2):
            for o in range(8):
                gs[it, h * 8 + o, 0] = grad[8 * o : 8 * o + 8, 128 * h : 128 * h + 128]
                gs[it, h * 8 + o, 1] = curv[8 * o : 8 * o + 8, 128 * h : 128 * h + 128]

        def g_send(t, carry, it=it):
            idx = lax.rem(me + t, 16)
            remote(gs.at[it, idx], gr.at[it, t - 1], s_send.at[8], s_g.at[it], rdev(idx)).start()
            return carry

        lax.fori_loop(1, 16, g_send, 0)
        wait_bytes(gr.at[it], s_g.at[it])
        tot = gs[it, me]
        for t in range(15):
            tot = tot + gr[it, t]
        bt[it + 1, c, r] = bt[it, c, r] + tot[0] / (1.0 + tot[1])
        mine = bt.at[it + 1, c, r]

        if last:
            def b_send(t, carry, mine=mine, it=it):
                dev = (lax.rem(r + t, 8), w)
                remote(mine, mine, s_send.at[9], s_b.at[it], dev).start()
                return carry

            lax.fori_loop(1, 8, b_send, 0)
            wait_bytes(gr.at[it, pl.ds(0, 7), 0], s_b.at[it])
        else:
            def b_send(t, carry, mine=mine, it=it):
                remote(mine, mine, s_send.at[9], s_b.at[it], rdev(lax.rem(me + t, 16))).start()
                return carry

            lax.fori_loop(1, 16, b_send, 0)
            wait_bytes(gr.at[it, :, 0], s_b.at[it])

    fac_out[...] = bt[ITERS, c].reshape(64, 128).T
    wait_bytes(at2.at[1 - c], s_sib)
    pltpu.make_async_copy(at2.at[1 - c], at_out.at[1 - c], s_out.at[1]).start()

    wait_bytes(bt.at[0, c], s_send.at[0])
    wait_bytes(cnt.at[c], s_send.at[1])
    wait_bytes(osend, s_send.at[2])
    wait_bytes(xs, s_send.at[3])
    wait_bytes(zs.at[:, pl.ds(0, 7)], s_send.at[4])
    wait_bytes(at1, s_send.at[5])
    wait_bytes(at1.at[pl.ds(0, 14)], s_send.at[6])
    wait_bytes(at2.at[c], s_send.at[7])
    wait_bytes(gr, s_send.at[8])
    wait_bytes(gr.at[0, :, 0], s_send.at[9])
    wait_bytes(gr.at[0, pl.ds(0, 7), 0], s_send.at[9])
    pltpu.make_async_copy(at2.at[c], at_out.at[c], s_out.at[0]).wait()
    pltpu.make_async_copy(at2.at[1 - c], at_out.at[1 - c], s_out.at[1]).wait()


def local(counts, offsets, loadings, factors):
    any_spec = pl.BlockSpec(memory_space=pl.ANY)
    vmem_spec = pl.BlockSpec(memory_space=pltpu.VMEM)
    dma = pltpu.SemaphoreType.DMA
    at_out, fac_out = pl.pallas_call(
        kernel,
        out_shape=(
            jax.ShapeDtypeStruct((2, 16, 64, 128), F32),
            jax.ShapeDtypeStruct((128, 64), F32),
        ),
        in_specs=[any_spec, any_spec, any_spec, vmem_spec],
        out_specs=(any_spec, vmem_spec),
        scratch_shapes=[
            pltpu.VMEM((2, 2, 8, 128, 128), jnp.int32),
            pltpu.VMEM((2, 2, 8, 128, 128), BF16),
            pltpu.VMEM((2, 2, 8, 128, 128), F32),
            pltpu.VMEM((2, 8, 128, 128), F32),
            pltpu.VMEM((16, 128, 64), F32),
            pltpu.VMEM((16, 128, 128), BF16),
            pltpu.VMEM((256, 256), BF16),
            pltpu.VMEM((256, 256), BF16),
            pltpu.VMEM((256, 256), BF16),
            pltpu.VMEM((256, 256), F32),
            pltpu.VMEM((256, 256), F32),
            pltpu.VMEM((ITERS + 1, 2, 8, 8, 128), F32),
            pltpu.VMEM((16, 64, 128), F32),
            pltpu.VMEM((2, 16, 64, 128), F32),
            pltpu.VMEM((ITERS, 8, 128, 128), F32),
            pltpu.VMEM((ITERS, 8, 128, 128), F32),
            pltpu.VMEM((8, 128, 128), F32),
            pltpu.VMEM((ITERS, 8, 128, 128), F32),
            pltpu.VMEM((ITERS, 7, 128, 128), F32),
            pltpu.VMEM((ITERS, 16, 2, 8, 128), F32),
            pltpu.VMEM((ITERS, 15, 2, 8, 128), F32),
            dma((3,)),
            dma((8,)),
            dma((8,)),
            dma,
            dma((10,)),
            dma((ITERS, 8)),
            dma((ITERS, 7)),
            dma((ITERS, 7)),
            dma((ITERS, 8)),
            dma((ITERS,)),
            dma((ITERS,)),
            dma,
            dma((2,)),
        ],
        compiler_params=pltpu.CompilerParams(
            collective_id=0, has_side_effects=True, vmem_limit_bytes=48 * 1024 * 1024
        ),
        name="glm_pca",
    )(
        counts.reshape(2, 2, 8, 128, 128),
        offsets.reshape(2, 2, 8, 128, 128),
        loadings.reshape(2, 16, 128, 64),
        factors,
    )
    new_loadings = at_out.reshape(32, 64, 128).transpose(0, 2, 1).reshape(4096, 64)
    return new_loadings, fac_out


def solution(mesh):
    placed = (P("rows", "weeks"), P("rows", "weeks"), P("rows", None), P("weeks", None))
    return jax.shard_map(
        local,
        mesh=mesh,
        in_specs=placed,
        out_specs=(P("rows", None), P("weeks", None)),
        check_vma=False,
    )
```

time: 697 us -> 105 us (0.15)
  waiting for transfers between devices: 634 us -> 0 us
  Pallas kernels: 0 us -> 98.2 us
  matrix products: 34.1 us -> 0 us
  between operations: 13.8 us -> 0.66 us
  other arithmetic: 10.2 us -> 0 us
    psum x4 -> x0, waiting for transfers between devices: 633 us -> none  [the longest x2 468 us: local(): total_a = lax.psum(stacked_a, 'weeks')]
    pallas_call x0 -> x1, Pallas kernels: none -> 98.2 us  [local(): pl.pallas_call(kernel, out_shape=(jax.ShapeDtypeStruct((2, 16, 64, 128),...]
    dot_general x12 -> x0, matrix products: 34.1 us -> none  [the longest x4 17.9 us: residuals(): eta = offsets_f + jnp.dot(load, fac.T, precision=HIGH)]
  transfers between devices with their start and end apart: 4 -> 0, of which waited for: 4 -> 0; matrix products, arithmetic and copies ran while one was open for 0% -> 0% of each run, Pallas kernels for 0% -> 0%
where the time goes in v1:
time: 105 us
  Pallas kernels  98.2 us (94%)
  local copies, waits for them, and re-layouts  5.92 us (6%)
    pallas_call x1, Pallas kernels, local(): pl.pallas_call(kernel, out_shape=(jax.ShapeDtypeStruct((2, 16, 64, 128),...  98.2 us
    unnamed x7, local copies, waits for them, and re-layouts  4.88 us

profile of v1, /device:TPU:1, one launch (start us, length us, event | category | flops | bytes accessed | tf_op | source)
XLA Modules:
  0.0 104.8 jit_solution(3582460558784686542)
XLA Ops:
  0.6 0.0 copy-start.1
  0.6 0.0 copy-start
  0.6 1.0 copy.7.fac
  1.7 3.2 %copy.6 = f32[4096,64]{1,0:T(8,128)} copy(f32[4096,64]{0,1:T(8,128)} %param.6) | data formatting | bytes 2097152 | tf_op args[2]
  4.8 0.0 copy-done.1
  4.8 0.0 copy-done
  4.8 98.2 %glm_pca.1 = (f32[2,16,64,128]{3,2,1,0:T(8,128)S(1)}, f32[128,64]{1,0:T(8,128)S(1)}) custom-call(s32[2,2,8,128,128]{4,3,2,1,0:T(8,128)S(1)} %bitcast.10, bf16[2,2,8,128,128]{4,3,2,1,0:T(8,128)(2,1)S(1)} %bitcast.12, f32[2,16,128,64]{3,2,1,0:T(8,128)} %bitcast.13, f32[128,64]{1,0:T(8,128)S(1)} %copy.7.fac), custom_call_target="tpu_custom_call" | custom-call | tf_op jit(solution)/shard_map/glm_pca/pallas_call | solution.py:289
  103.1 1.0 copy.12
  104.1 0.7 copy.9
Async XLA Ops:
  0.6 4.2 %copy-start.1 = (bf16[4096,128]{1,0:T(8,128)(2,1)S(1)}, bf16[4096,128]{1,0:T(8,128)(2,1)}, u32[]{:S(2)}) copy-start(bf16[4096,128]{1,0:T(8,128)(2,1)} %param.5) | copy-start | bytes 3145732
  0.6 4.2 %copy-start = (s32[4096,128]{1,0:T(8,128)S(1)}, s32[4096,128]{1,0:T(8,128)}, u32[]{:S(2)}) copy-start(s32[4096,128]{1,0:T(8,128)} %param.4) | copy-start | bytes 6291460

commit v2 on v1

--- a/solution.py
+++ b/solution.py
@@ -11,8 +11,17 @@
 F32 = jnp.float32
 BF16 = jnp.bfloat16
 MESH = pl.DeviceIdType.MESH
-NZ = 8
-R = 8
+LATE = 3
+LAG = 5
+STAG = 1
+
+
+def pack(digits):
+    return sum(d * 8**i for i, d in enumerate(digits))
+
+
+OWNERS = pack([4, 2, 6, 5, 3, 1, 7, 0])
+TARGETS = pack([1, 1, 7, 5, 3, 1, 7])
 
 
 def far_first(j):
@@ -50,8 +59,11 @@
     def rdev(idx):
         return (lax.rem(idx, 8), w - c + lax.div(idx, 8))
 
-    def zsrc(j):
-        return lax.rem(z + 8 - far_first(j), 8)
+    def zdst(seq):
+        return lax.rem(z + lax.rem(seq, 8), 8)
+
+    def zsrc(f):
+        return lax.rem(z + 8 - far_first(f), 8)
 
     def remote(src, dst, ss, rs, dev):
         return pltpu.make_async_remote_copy(
@@ -61,6 +73,11 @@
     def wait_bytes(ref, sem):
         pltpu.make_async_copy(ref, ref, sem).wait()
 
+    def put(h, b, carry):
+        cols = pl.ds(pl.multiple_of((h * 16 + b) * 128, 128), 128)
+        pltpu.make_async_copy(at2.at[h, b], at_out.at[:, cols], s_out).start()
+        return carry
+
     me = c * 8 + r
     barrier = pltpu.get_barrier_semaphore()
 
@@ -74,7 +91,7 @@
 
     ld_off = pltpu.make_async_copy(offs, obf, s_loc.at[0])
     ld_cnt = pltpu.make_async_copy(counts.at[c], cnt.at[c], s_loc.at[1])
-    ld_a0 = pltpu.make_async_copy(load.at[c], a0, s_loc.at[2])
+    ld_a0 = pltpu.make_async_copy(load.at[:, pl.ds(c * 2048, 2048)], a0, s_loc.at[2])
     ld_off.start()
     ld_a0.start()
     ld_cnt.start()
@@ -82,37 +99,42 @@
     lax.fori_loop(1, 16, greet_r, 0)
     pl.semaphore_signal(barrier, inc=1, device_id=xp, device_id_type=MESH)
 
-    bt[0, c] = fac[...].T.reshape(8, 8, 128)
+    bt[0, c] = fac[...].reshape(8, 8, 128)
+
+    def first(b):
+        return a0[:, pl.ds(pl.multiple_of(b * 128, 128), 128)]
+
+    def stack(hi, lo):
+        return jnp.concatenate([hi.astype(F32), lo.astype(F32)], axis=0).T.astype(BF16)
+
     ld_off.wait()
-    pl.semaphore_wait(barrier, 23)
-
-    remote(bt.at[0, c], bt.at[0, c], s_send.at[0], s_bt, sib).start()
-
-    def swap(j, carry):
-        d = lax.rem(z + far_first(j), 8)
-        remote(counts.at[1 - c, :, d], cnt.at[c, :, d], s_send.at[1], s_cnt.at[j], sib).start()
+
+    def widen(d, carry):
         for x in range(2):
             osend[x, d] = obf[1 - c, x, d].astype(F32)
-        remote(osend.at[:, d], off.at[c, :, d], s_send.at[2], s_off.at[j], sib).start()
-        return carry
-
-    lax.fori_loop(0, 8, swap, 0)
-
-    def prepare(d, carry):
-        for x in range(2):
             off[c, x, d] = obf[c, x, d].astype(F32)
         return carry
 
-    lax.fori_loop(0, 8, prepare, 0)
+    lax.fori_loop(0, 8, widen, 0)
     ld_a0.wait()
 
     def first_x(b, carry):
-        hi, lo = split(a0[b])
-        xmat[b] = jnp.concatenate([hi.astype(F32), lo.astype(F32)], axis=1).astype(BF16)
+        xmat[b] = stack(*split(first(b)))
         return carry
 
     lax.fori_loop(0, 16, first_x, 0)
     ld_cnt.wait()
+    pl.semaphore_wait(barrier, 23)
+
+    remote(bt.at[0, c], bt.at[0, c], s_send.at[0], s_bt, sib).start()
+
+    def swap(k, seq):
+        d = zdst(seq)
+        remote(counts.at[1 - c, :, d], cnt.at[c, :, d], s_send.at[1], s_cnt.at[k], sib).start()
+        remote(osend.at[:, d], off.at[c, :, d], s_send.at[2], s_off.at[k], sib).start()
+        return lax.div(seq, 8)
+
+    lax.fori_loop(0, 8, swap, OWNERS)
 
     def week_weights(it):
         b = jnp.concatenate([bt[it, 0].reshape(64, 128), bt[it, 1].reshape(64, 128)], axis=1)
@@ -142,7 +164,7 @@
         a = at[x * 8 + d]
         hi, lo = split(a)
         ph, pw = split(a * a)
-        xmat[x * 8 + d] = jnp.concatenate([hi.astype(F32), lo.astype(F32)], axis=0).T.astype(BF16)
+        xmat[x * 8 + d] = stack(hi, lo)
         rh, rl, n = residual(x, d)
         lt = jnp.concatenate([hi, -ph, lo, -pw], axis=0)
         g1[...] += mm(lt, rh)
@@ -156,76 +178,105 @@
             pltpu.make_async_copy(bt.at[0, 1 - c], bt.at[0, 1 - c], s_bt).wait()
         week_weights(it)
 
-        def a_step(j, carry, it=it):
+        def finish(it=it, at=at):
+            def z_sum(f, total):
+                wait_bytes(zr.at[it, f], s_z.at[it, f])
+                return total + zr[it, f]
+
+            total = lax.fori_loop(3, 7, z_sum, zs[it, 7]).T
+            old = first(own) if it == 0 else at1[own]
+            at[own] = old + total[:64] / (1.0 + total[64:])
+
+            def ag_send(f, carry):
+                remote(at.at[own], at.at[own], s_send.at[6], s_agz.at[it, f], zdev(far_first(f))).start()
+                return carry
+
+            lax.fori_loop(0, 7, ag_send, 0)
+            remote(at.at[own], at.at[own], s_send.at[5], s_agx.at[it, 7], xp).start()
+
+        def emit(j, d, x, it=it):
+            v = left(x, d)
+
+            @pl.when(x == xl)
+            def _():
+                so[j] = v
+
+            @pl.when(x != xl)
+            def _():
+                xs[it, j] = v
+                remote(xs.at[it, j], xr.at[it, j], s_send.at[3], s_x.at[it, j], xp).start()
+
+        def a_one(j, seq, it=it, emit=emit):
+            d = zdst(seq)
+            if it == 0:
+                wait_bytes(cnt.at[1 - c, :, d], s_cnt.at[j])
+                wait_bytes(off.at[1 - c, :, d], s_off.at[j])
+            emit(j, d, lax.rem(xl + 1 + c * STAG, 2))
+            return lax.div(seq, 8)
+
+        def a_two(j, carry, it=it, emit=emit):
+            seq, target = carry
+
             @pl.when(j < 8)
             def _():
-                d = lax.rem(z + far_first(j), 8)
-                if it == 0:
-                    wait_bytes(cnt.at[1 - c, :, d], s_cnt.at[j])
-                    wait_bytes(off.at[1 - c, :, d], s_off.at[j])
-                xs[it, j] = left(1 - xl, d)
-                remote(xs.at[it, j], xr.at[it, j], s_send.at[3], s_x.at[it, j], xp).start()
-                so[j] = left(xl, d)
-
-            @pl.when(j >= 3)
-            def _():
-                k = j - 3
-                wait_bytes(xr.at[it, k], s_x.at[it, k])
-                zs[it, k] = so[k] + xr[it, k]
-
-                @pl.when(k < 7)
+                emit(j, zdst(seq), lax.rem(xl + c * STAG, 2))
+
+            f = j - LATE * c * STAG
+
+            @pl.when((f >= 0) & (f < 8))
+            def _():
+                wait_bytes(xr.at[it, f], s_x.at[it, f])
+                zs[it, f] = so[f] + xr[it, f]
+
+                @pl.when((f >= 4) & (f < 7))
+                def _():
+                    wait_bytes(zr.at[it, f - 4], s_z.at[it, f - 4])
+                    zs[it, f] += zr[it, f - 4]
+
+                @pl.when(f < 7)
                 def _():
                     remote(
-                        zs.at[it, k], zr.at[it, k], s_send.at[4], s_z.at[it, k], zdev(far_first(k))
+                        zs.at[it, f], zr.at[it, f], s_send.at[4], s_z.at[it, f], zdev(lax.rem(target, 8))
                     ).start()
 
-            return carry
-
-        lax.fori_loop(0, 11, a_step, 0)
-
-        def z_sum(k, total, it=it):
-            wait_bytes(zr.at[it, k], s_z.at[it, k])
-            return total + zr[it, k]
-
-        total = lax.fori_loop(0, 7, z_sum, zs[it, 7]).T
-        old = a0[own].T if it == 0 else at1[own]
-        at[own] = old + total[:64] / (1.0 + total[64:])
-
-        remote(at.at[own], at.at[own], s_send.at[5], s_agx.at[it, 7], xp).start()
-
-        def ag_send(j, carry, it=it, at=at):
-            remote(at.at[own], at.at[own], s_send.at[6], s_agz.at[it, j], zdev(far_first(j))).start()
-            return carry
-
-        lax.fori_loop(0, 7, ag_send, 0)
+            return lax.div(seq, 8), lax.div(target, 8)
+
+        lax.fori_loop(0, 8, a_one, OWNERS)
+        delayed = TARGETS * (1 + c * STAG * (8**LATE - 1))
+        lax.fori_loop(0, 8 + LATE * STAG, a_two, (jnp.int32(OWNERS), delayed))
+        finish()
 
         g1[...] = jnp.zeros_like(g1)
         g2[...] = jnp.zeros_like(g2)
-        right(at, xl, z)
 
         def b_step(k, carry, it=it, at=at):
-            @pl.when(k < 7)
-            def _():
-                d = zsrc(k)
-                blk = at.at[xl * 8 + d]
-                wait_bytes(blk, s_agz.at[it, k])
-                remote(blk, blk, s_send.at[5], s_agx.at[it, k], xp).start()
+            @pl.when(k < 8)
+            def _():
+                f = k
+                d = zsrc(f)
+
+                @pl.when(f < 7)
+                def _():
+                    blk = at.at[xl * 8 + d]
+                    wait_bytes(blk, s_agz.at[it, f])
+                    remote(blk, blk, s_send.at[5], s_agx.at[it, f], xp).start()
+
                 right(at, xl, d)
 
-            @pl.when(k >= 2)
-            def _():
-                k2 = lax.rem(k + 5, 8)
-                d = zsrc(k2)
-                wait_bytes(at.at[(1 - xl) * 8 + d], s_agx.at[it, k2])
+            @pl.when(k >= LAG)
+            def _():
+                f = k - LAG
+                d = zsrc(f)
+                wait_bytes(at.at[(1 - xl) * 8 + d], s_agx.at[it, f])
                 right(at, 1 - xl, d)
 
             return carry
 
-        lax.fori_loop(0, 10, b_step, 0)
+        lax.fori_loop(0, 8 + LAG, b_step, 0)
 
         if last:
             remote(at2.at[c], at2.at[c], s_send.at[7], s_sib, sib).start()
-            pltpu.make_async_copy(at2.at[c], at_out.at[c], s_out.at[0]).start()
+            lax.fori_loop(0, 16, functools.partial(put, c), 0)
 
         grad = g1[0:64] + g1[128:192] + g2[0:64]
         curv = g1[64:128] + g1[192:256] + g2[64:128] + g2[128:192] + g2[192:256]
@@ -263,9 +314,9 @@
             lax.fori_loop(1, 16, b_send, 0)
             wait_bytes(gr.at[it, :, 0], s_b.at[it])
 
-    fac_out[...] = bt[ITERS, c].reshape(64, 128).T
+    fac_out[...] = bt[ITERS, c].reshape(64, 128)
     wait_bytes(at2.at[1 - c], s_sib)
-    pltpu.make_async_copy(at2.at[1 - c], at_out.at[1 - c], s_out.at[1]).start()
+    lax.fori_loop(0, 16, functools.partial(put, 1 - c), 0)
 
     wait_bytes(bt.at[0, c], s_send.at[0])
     wait_bytes(cnt.at[c], s_send.at[1])
@@ -278,19 +329,33 @@
     wait_bytes(gr, s_send.at[8])
     wait_bytes(gr.at[0, :, 0], s_send.at[9])
     wait_bytes(gr.at[0, pl.ds(0, 7), 0], s_send.at[9])
-    pltpu.make_async_copy(at2.at[c], at_out.at[c], s_out.at[0]).wait()
-    pltpu.make_async_copy(at2.at[1 - c], at_out.at[1 - c], s_out.at[1]).wait()
+    wait_bytes(at2, s_out)
+
+
+def hand_over(a_ref, f_ref, a_out, f_out, a_buf, f_buf, sem_in, sem_out):
+    parts = [(f_ref, f_buf, f_out)]
+    for i in range(4):
+        rows = pl.ds(16 * i, 16)
+        parts.append((a_ref.at[rows], a_buf.at[rows], a_out.at[rows]))
+    for i, (src, buf, _) in enumerate(parts):
+        pltpu.make_async_copy(src, buf, sem_in.at[i]).start()
+    for i, (src, buf, dst) in enumerate(parts):
+        pltpu.make_async_copy(src, buf, sem_in.at[i]).wait()
+        pltpu.make_async_copy(buf, dst, sem_out.at[i]).start()
+    for i, (_, buf, dst) in enumerate(parts):
+        pltpu.make_async_copy(buf, dst, sem_out.at[i]).wait()
 
 
 def local(counts, offsets, loadings, factors):
     any_spec = pl.BlockSpec(memory_space=pl.ANY)
+    hbm_spec = pl.BlockSpec(memory_space=pltpu.HBM)
     vmem_spec = pl.BlockSpec(memory_space=pltpu.VMEM)
     dma = pltpu.SemaphoreType.DMA
     at_out, fac_out = pl.pallas_call(
         kernel,
         out_shape=(
-            jax.ShapeDtypeStruct((2, 16, 64, 128), F32),
-            jax.ShapeDtypeStruct((128, 64), F32),
+            jax.ShapeDtypeStruct((64, 4096), F32),
+            jax.ShapeDtypeStruct((64, 128), F32),
         ),
         in_specs=[any_spec, any_spec, any_spec, vmem_spec],
         out_specs=(any_spec, vmem_spec),
@@ -299,7 +364,7 @@
             pltpu.VMEM((2, 2, 8, 128, 128), BF16),
             pltpu.VMEM((2, 2, 8, 128, 128), F32),
             pltpu.VMEM((2, 8, 128, 128), F32),
-            pltpu.VMEM((16, 128, 64), F32),
+            pltpu.VMEM((64, 2048), F32),
             pltpu.VMEM((16, 128, 128), BF16),
             pltpu.VMEM((256, 256), BF16),
             pltpu.VMEM((256, 256), BF16),
@@ -328,20 +393,30 @@
             dma((ITERS,)),
             dma((ITERS,)),
             dma,
-            dma((2,)),
+            dma,
         ],
         compiler_params=pltpu.CompilerParams(
-            collective_id=0, has_side_effects=True, vmem_limit_bytes=48 * 1024 * 1024
+            collective_id=0, has_side_effects=True, vmem_limit_bytes=60 * 1024 * 1024
         ),
         name="glm_pca",
     )(
         counts.reshape(2, 2, 8, 128, 128),
         offsets.reshape(2, 2, 8, 128, 128),
-        loadings.reshape(2, 16, 128, 64),
-        factors,
+        loadings.T,
+        factors.T,
     )
-    new_loadings = at_out.reshape(32, 64, 128).transpose(0, 2, 1).reshape(4096, 64)
-    return new_loadings, fac_out
+    at_out, fac_out = pl.pallas_call(
+        hand_over,
+        out_shape=(
+            jax.ShapeDtypeStruct((64, 4096), F32),
+            jax.ShapeDtypeStruct((64, 128), F32),
+        ),
+        in_specs=[hbm_spec, hbm_spec],
+        out_specs=(hbm_spec, hbm_spec),
+        scratch_shapes=[pltpu.VMEM((64, 4096), F32), pltpu.VMEM((64, 128), F32), dma((5,)), dma((5,))],
+        name="hand_over",
+    )(at_out, fac_out)
+    return at_out.T, fac_out.T
 
 
 def solution(mesh):

time: 105 us -> 97.2 us (0.926)
  local copies, waits for them, and re-layouts: 5.92 us -> 0 us
  Pallas kernels: 98.2 us -> 96.4 us
    unnamed x7 -> x0, local copies, waits for them, and re-layouts: 4.88 us -> none
    pallas_call x1 -> x2, Pallas kernels: 98.2 us -> 96.4 us  [the longest x1 94.4 us: local(): pl.pallas_call(kernel, out_shape=(jax.ShapeDtypeStruct((64, 4096), F32),...]
where the time goes in v2:
time: 97.2 us; the launch traced here: 97 us
  Pallas kernels  96.4 us (99%)
    pallas_call x1, Pallas kernels, local(): pl.pallas_call(kernel, out_shape=(jax.ShapeDtypeStruct((64, 4096), F32),...  94.4 us
    pallas_call x1, Pallas kernels, local(): pl.pallas_call(hand_over, out_shape=(jax.ShapeDtypeStruct((64, 4096), F32...  2.02 us

profile of v2, /device:TPU:1, one launch (start us, length us, event | category | flops | bytes accessed | tf_op | source)
XLA Modules:
  0.0 97.0 jit_solution(16393461658349545568)
XLA Ops:
  0.6 94.4 %glm_pca.1 = (f32[64,4096]{1,0:T(8,128)}, f32[64,128]{1,0:T(8,128)}) custom-call(s32[2,2,8,128,128]{4,3,2,1,0:T(8,128)} %bitcast.6, bf16[2,2,8,128,128]{4,3,2,1,0:T(8,128)(2,1)} %bitcast.7, f32[64,4096]{1,0:T(8,128)} %bitcast.8, f32[64,128]{1,0:T(8,128)} %bitcast.9), custom_call_target="tpu_custom_call" | custom-call | tf_op jit(solution)/shard_map/glm_pca/pallas_call | solution.py:354
  95.0 2.0 %hand_over.1 = (f32[64,4096]{1,0:T(8,128)}, f32[64,128]{1,0:T(8,128)}) custom-call(f32[64,4096]{1,0:T(8,128)} %get-tuple-element.6.a_ref, f32[64,128]{1,0:T(8,128)} %get-tuple-element.7.f_ref), custom_call_target="tpu_custom_call" | custom-call | tf_op jit(solution)/shard_map/hand_over/pallas_call | solution.py:408

commit v3 on v2

--- a/solution.py
+++ b/solution.py
@@ -22,6 +22,7 @@
 
 OWNERS = pack([4, 2, 6, 5, 3, 1, 7, 0])
 TARGETS = pack([1, 1, 7, 5, 3, 1, 7])
+OUTWARD = pack([0, 1, 7, 3, 5, 2, 6, 4])
 
 
 def far_first(j):
@@ -187,11 +188,13 @@
             old = first(own) if it == 0 else at1[own]
             at[own] = old + total[:64] / (1.0 + total[64:])
 
-            def ag_send(f, carry):
-                remote(at.at[own], at.at[own], s_send.at[6], s_agz.at[it, f], zdev(far_first(f))).start()
-                return carry
-
-            lax.fori_loop(0, 7, ag_send, 0)
+            def ag_send(p, seq):
+                remote(
+                    at.at[own], at.at[own], s_send.at[6], s_agz.at[it, p], zdev(lax.rem(seq, 8))
+                ).start()
+                return lax.div(seq, 8)
+
+            lax.fori_loop(0, 4, ag_send, OUTWARD // 8)
             remote(at.at[own], at.at[own], s_send.at[5], s_agx.at[it, 7], xp).start()
 
         def emit(j, d, x, it=it):
@@ -250,29 +253,36 @@
         g2[...] = jnp.zeros_like(g2)
 
         def b_step(k, carry, it=it, at=at):
+            seq, late = carry
+
             @pl.when(k < 8)
             def _():
-                f = k
-                d = zsrc(f)
-
-                @pl.when(f < 7)
+                d = lax.rem(z + 8 - lax.rem(seq, 8), 8)
+
+                @pl.when(k > 0)
                 def _():
+                    p = k - 1
                     blk = at.at[xl * 8 + d]
-                    wait_bytes(blk, s_agz.at[it, f])
-                    remote(blk, blk, s_send.at[5], s_agx.at[it, f], xp).start()
+                    wait_bytes(blk, s_agz.at[it, p])
+
+                    @pl.when(p < 3)
+                    def _():
+                        on = 1 + 6 * lax.rem(p, 2)
+                        remote(blk, blk, s_send.at[6], s_agz.at[it, p + 4], zdev(on)).start()
+
+                    remote(blk, blk, s_send.at[5], s_agx.at[it, p], xp).start()
 
                 right(at, xl, d)
 
             @pl.when(k >= LAG)
             def _():
-                f = k - LAG
-                d = zsrc(f)
-                wait_bytes(at.at[(1 - xl) * 8 + d], s_agx.at[it, f])
+                d = lax.rem(z + 8 - lax.rem(late, 8), 8)
+                wait_bytes(at.at[(1 - xl) * 8 + d], s_agx.at[it, lax.rem(k + 7 - LAG, 8)])
                 right(at, 1 - xl, d)
 
-            return carry
-
-        lax.fori_loop(0, 8 + LAG, b_step, 0)
+            return lax.div(seq, 8), lax.select(k >= LAG, lax.div(late, 8), late)
+
+        lax.fori_loop(0, 8 + LAG, b_step, (jnp.int32(OUTWARD), jnp.int32(OUTWARD)))
 
         if last:
             remote(at2.at[c], at2.at[c], s_send.at[7], s_sib, sib).start()
@@ -286,8 +296,9 @@
                 gs[it, h * 8 + o, 1] = curv[8 * o : 8 * o + 8, 128 * h : 128 * h + 128]
 
         def g_send(t, carry, it=it):
-            idx = lax.rem(me + t, 16)
-            remote(gs.at[it, idx], gr.at[it, t - 1], s_send.at[8], s_g.at[it], rdev(idx)).start()
+            u = 1 + lax.rem(t + 3, 15)
+            idx = lax.rem(me + u, 16)
+            remote(gs.at[it, idx], gr.at[it, u - 1], s_send.at[8], s_g.at[it], rdev(idx)).start()
             return carry
 
         lax.fori_loop(1, 16, g_send, 0)
@@ -308,7 +319,7 @@
             wait_bytes(gr.at[it, pl.ds(0, 7), 0], s_b.at[it])
         else:
             def b_send(t, carry, mine=mine, it=it):
-                remote(mine, mine, s_send.at[9], s_b.at[it], rdev(lax.rem(me + t, 16))).start()
+                remote(mine, mine, s_send.at[9], s_b.at[it], rdev(lax.rem(me + 1 + lax.rem(t + 3, 15), 16))).start()
                 return carry
 
             lax.fori_loop(1, 16, b_send, 0)

time: 97.2 us -> 92.9 us (0.956)
  Pallas kernels: 96.4 us -> 92.1 us
    pallas_call x1, Pallas kernels: 94.4 us -> 90 us  [local(): pl.pallas_call(kernel, out_shape=(jax.ShapeDtypeStruct((64, 4096), F32),...]
where the time goes in v3:
time: 92.9 us; the launch traced here: 92.7 us
  Pallas kernels  92.1 us (99%)
    pallas_call x1, Pallas kernels, local(): pl.pallas_call(kernel, out_shape=(jax.ShapeDtypeStruct((64, 4096), F32),...  90 us
    pallas_call x1, Pallas kernels, local(): pl.pallas_call(hand_over, out_shape=(jax.ShapeDtypeStruct((64, 4096), F32...  2.02 us

profile of v3, /device:TPU:1, one launch (start us, length us, event | category | flops | bytes accessed | tf_op | source)
XLA Modules:
  0.0 92.7 jit_solution(14615902798768345874)
XLA Ops:
  0.6 90.0 %glm_pca.1 = (f32[64,4096]{1,0:T(8,128)}, f32[64,128]{1,0:T(8,128)}) custom-call(s32[2,2,8,128,128]{4,3,2,1,0:T(8,128)} %bitcast.6, bf16[2,2,8,128,128]{4,3,2,1,0:T(8,128)(2,1)} %bitcast.7, f32[64,4096]{1,0:T(8,128)} %bitcast.8, f32[64,128]{1,0:T(8,128)} %bitcast.9), custom_call_target="tpu_custom_call" | custom-call | tf_op jit(solution)/shard_map/glm_pca/pallas_call | solution.py:365
  90.7 2.0 %hand_over.1 = (f32[64,4096]{1,0:T(8,128)}, f32[64,128]{1,0:T(8,128)}) custom-call(f32[64,4096]{1,0:T(8,128)} %get-tuple-element.6.a_ref, f32[64,128]{1,0:T(8,128)} %get-tuple-element.7.f_ref), custom_call_target="tpu_custom_call" | custom-call | tf_op jit(solution)/shard_map/hand_over/pallas_call | solution.py:419

commit v4 on v3

--- a/solution.py
+++ b/solution.py
@@ -93,14 +93,15 @@
     ld_off = pltpu.make_async_copy(offs, obf, s_loc.at[0])
     ld_cnt = pltpu.make_async_copy(counts.at[c], cnt.at[c], s_loc.at[1])
     ld_a0 = pltpu.make_async_copy(load.at[:, pl.ds(c * 2048, 2048)], a0, s_loc.at[2])
+    ld_fac = pltpu.make_async_copy(fac, bt.at[0, c], s_loc.at[3])
     ld_off.start()
+    ld_fac.start()
     ld_a0.start()
     ld_cnt.start()
     lax.fori_loop(1, 8, greet_z, 0)
     lax.fori_loop(1, 16, greet_r, 0)
     pl.semaphore_signal(barrier, inc=1, device_id=xp, device_id_type=MESH)
 
-    bt[0, c] = fac[...].reshape(8, 8, 128)
 
     def first(b):
         return a0[:, pl.ds(pl.multiple_of(b * 128, 128), 128)]
@@ -125,6 +126,7 @@
 
     lax.fori_loop(0, 16, first_x, 0)
     ld_cnt.wait()
+    ld_fac.wait()
     pl.semaphore_wait(barrier, 23)
 
     remote(bt.at[0, c], bt.at[0, c], s_send.at[0], s_bt, sib).start()
@@ -343,18 +345,15 @@
     wait_bytes(at2, s_out)
 
 
-def hand_over(a_ref, f_ref, a_out, f_out, a_buf, f_buf, sem_in, sem_out):
-    parts = [(f_ref, f_buf, f_out)]
+def hand_over(a_ref, f_ref, a_out, f_out, sem):
+    moves = [pltpu.make_async_copy(f_ref, f_out, sem.at[4])]
     for i in range(4):
         rows = pl.ds(16 * i, 16)
-        parts.append((a_ref.at[rows], a_buf.at[rows], a_out.at[rows]))
-    for i, (src, buf, _) in enumerate(parts):
-        pltpu.make_async_copy(src, buf, sem_in.at[i]).start()
-    for i, (src, buf, dst) in enumerate(parts):
-        pltpu.make_async_copy(src, buf, sem_in.at[i]).wait()
-        pltpu.make_async_copy(buf, dst, sem_out.at[i]).start()
-    for i, (_, buf, dst) in enumerate(parts):
-        pltpu.make_async_copy(buf, dst, sem_out.at[i]).wait()
+        moves.append(pltpu.make_async_copy(a_ref.at[rows], a_out.at[rows], sem.at[i]))
+    for move in moves:
+        move.start()
+    for move in moves:
+        move.wait()
 
 
 def local(counts, offsets, loadings, factors):
@@ -368,7 +367,7 @@
             jax.ShapeDtypeStruct((64, 4096), F32),
             jax.ShapeDtypeStruct((64, 128), F32),
         ),
-        in_specs=[any_spec, any_spec, any_spec, vmem_spec],
+        in_specs=[any_spec, any_spec, any_spec, hbm_spec],
         out_specs=(any_spec, vmem_spec),
         scratch_shapes=[
             pltpu.VMEM((2, 2, 8, 128, 128), jnp.int32),
@@ -392,7 +391,7 @@
             pltpu.VMEM((ITERS, 7, 128, 128), F32),
             pltpu.VMEM((ITERS, 16, 2, 8, 128), F32),
             pltpu.VMEM((ITERS, 15, 2, 8, 128), F32),
-            dma((3,)),
+            dma((4,)),
             dma((8,)),
             dma((8,)),
             dma,
@@ -407,14 +406,14 @@
             dma,
         ],
         compiler_params=pltpu.CompilerParams(
-            collective_id=0, has_side_effects=True, vmem_limit_bytes=60 * 1024 * 1024
+            collective_id=0, has_side_effects=True, vmem_limit_bytes=52 * 1024 * 1024
         ),
         name="glm_pca",
     )(
         counts.reshape(2, 2, 8, 128, 128),
         offsets.reshape(2, 2, 8, 128, 128),
         loadings.T,
-        factors.T,
+        factors.T.reshape(8, 8, 128),
     )
     at_out, fac_out = pl.pallas_call(
         hand_over,
@@ -422,9 +421,10 @@
             jax.ShapeDtypeStruct((64, 4096), F32),
             jax.ShapeDtypeStruct((64, 128), F32),
         ),
-        in_specs=[hbm_spec, hbm_spec],
+        in_specs=[any_spec, any_spec],
         out_specs=(hbm_spec, hbm_spec),
-        scratch_shapes=[pltpu.VMEM((64, 4096), F32), pltpu.VMEM((64, 128), F32), dma((5,)), dma((5,))],
+        scratch_shapes=[dma((5,))],
+        compiler_params=pltpu.CompilerParams(vmem_limit_bytes=1024 * 1024),
         name="hand_over",
     )(at_out, fac_out)
     return at_out.T, fac_out.T

time: 92.9 us -> 91 us (0.980)
  Pallas kernels: 92.1 us -> 89.4 us
    pallas_call x1, Pallas kernels: 90 us -> 88.4 us  [local(): pl.pallas_call(kernel, out_shape=(jax.ShapeDtypeStruct((64, 4096), F32),...]
    pallas_call x1, Pallas kernels: 2.02 us -> 1.02 us  [local(): pl.pallas_call(hand_over, out_shape=(jax.ShapeDtypeStruct((64, 4096), F32...]
where the time goes in v4:
time: 91 us; the launch traced here: 90.8 us
  Pallas kernels  89.4 us (98%)
    pallas_call x1, Pallas kernels, local(): pl.pallas_call(kernel, out_shape=(jax.ShapeDtypeStruct((64, 4096), F32),...  88.4 us

profile of v4, /device:TPU:1, one launch (start us, length us, event | category | flops | bytes accessed | tf_op | source)
XLA Modules:
  0.0 90.8 jit_solution(10013952211284836257)
XLA Ops:
  0.6 0.0 copy-start
  0.6 0.7 copy-done
  1.4 88.4 %glm_pca.1 = (f32[64,4096]{1,0:T(8,128)S(1)}, f32[64,128]{1,0:T(8,128)S(1)}) custom-call(s32[2,2,8,128,128]{4,3,2,1,0:T(8,128)} %bitcast.9, bf16[2,2,8,128,128]{4,3,2,1,0:T(8,128)(2,1)} %bitcast.10, f32[64,4096]{1,0:T(8,128)} %bitcast.11, f32[8,8,128]{2,1,0:T(8,128)S(1)} %bitcast.8), custom_call_target="tpu_custom_call" | custom-call | tf_op jit(solution)/shard_map/glm_pca/pallas_call | solution.py:364
  89.8 1.0 %hand_over.1 = (f32[64,4096]{1,0:T(8,128)}, f32[64,128]{1,0:T(8,128)}) custom-call(f32[64,4096]{1,0:T(8,128)S(1)} %get-tuple-element.6.a_ref, f32[64,128]{1,0:T(8,128)S(1)} %get-tuple-element.7.f_ref), custom_call_target="tpu_custom_call" | custom-call | tf_op jit(solution)/shard_map/hand_over/pallas_call | solution.py:418
Async XLA Ops:
  0.6 0.8 copy-start
